TPU v7x, 32 devices: a whole 2x2x4 slice. The times are simulated.
32 devices in a mesh: tm: 4 (over z), chan: 8 (over y, x, core).
Axes of the slice: x: 2, y: 2, z: 4, core: 2. Of those that a mesh axis runs over, the one named last changes fastest.
Arguments:
- voltages: bfloat16 [512, 1024, 1024], P('chan', None, 'tm'), may hold values from -4 to 4
- exponents: int32 [512, 16, 4], P('chan', None, 'tm'), may hold values from -2 to 2
- gain_real: float32 [512, 1024], P(None, 'chan'), may hold values from 0.1 to 1.9
- gain_imag: float32 [512, 1024], P(None, 'chan'), may hold values from -1.5 to 1.5
- delays: float32 [512, 256], replicated, may hold values from -8 to 8
- filter_taps: float32 [4, 1024], replicated, may hold values from -3 to 3
Outputs:
- beam_series: bfloat16 [256, 1024, 1024], P('chan', None, 'tm')
All inputs are finite; a program needn't handle non-finite values.
Results may differ from a plain program's by a relative error of at most 0.0062.
Values may be sent and summed in bfloat16 or wider, within the bound.
A program may use at most 320 MiB of HBM per device.

v0:
```python
import functools
import math

import jax
import jax.numpy as jnp
from jax import lax
from jax.experimental import pallas as pl
from jax.experimental.pallas import tpu as pltpu
from jax.sharding import PartitionSpec as P

TWO_PI = 6.283185307179586
SETS = 2
QUAD = 4
VMEM_LIMIT = 60 * 1024 * 1024


def radix_of(chunk_channels):
    return max(r for r in (4, 2, 1) if chunk_channels % r == 0 and (chunk_channels // r) % 16 == 0 or r == 1)


def chip_grid(devices):
    cores = 2 if devices % 2 == 0 else 1
    chips = devices // cores
    rows = max(r for r in range(1, chips + 1) if chips % r == 0 and r * r <= chips)
    return rows, chips // rows, cores


def synthesis_tables(channels, devices, chunk_channels, radix):
    span = channels // radix
    per = chunk_channels // radix
    local = SETS * chunk_channels
    shape = (radix, span, span)
    residue = lax.broadcasted_iota(jnp.int32, shape, 0)
    sample = lax.broadcasted_iota(jnp.int32, shape, 1)
    place = lax.broadcasted_iota(jnp.int32, shape, 2)
    chunk = place // (devices * per)
    source = place // per % devices
    channel = source * local + chunk * chunk_channels + place % per * radix + residue
    phases = TWO_PI / channels * (channel * sample % channels).astype(jnp.float32)
    normalizer = 1.0 / math.sqrt(channels)
    cosine = (jnp.cos(phases) * normalizer).astype(jnp.bfloat16)
    sine = (jnp.sin(phases) * normalizer).astype(jnp.bfloat16)
    return jnp.concatenate([cosine, sine], axis=2)


class Side:
    def __init__(self, which, grid):
        self.rows, self.cols, self.cores = grid
        self.which = which
        self.group, self.reduce = (self.rows, self.cols) if which == 0 else (self.cols, self.rows)
        self.slots = self.group * self.cores

    def device(self, e, r, k):
        i, j = (e, r) if self.which == 0 else (r, e)
        return (i * self.cols + j) * self.cores + k

    def place(self):
        d = lax.axis_index("chan")
        k = d % self.cores
        j = d // self.cores % self.cols
        i = d // (self.cores * self.cols)
        return (i, j, k) if self.which == 0 else (j, i, k)

    def peer(self, off):
        e, r, k = self.place()
        e2 = (e + off // self.cores) % self.group
        k2 = (k + off % self.cores) % self.cores
        return e2 * self.cores + k2, self.device(e2, r, k2), e2, k2


def exchange_kernel(grid, n_taps, channels, radix, *refs):
    sides = [Side(s, grid) for s in range(SETS)]
    v = refs[0]
    gains, factors, delays = refs[1:3], refs[3:5], refs[5:7]
    spec, halo, raw, part, got, done, ends = (refs[7 + 2 * n : 9 + 2 * n] for n in range(7))
    scratch = refs[21:]
    xv, xf_re, xf_im, w_re, w_im, st_c, st_s = scratch[:7]
    s_re, s_im, ob, pa, pb, hal, hb, zero = scratch[7:15]
    gbuf, fbuf, fsum, rot_c, rot_s, dv = (scratch[15 + 2 * n : 17 + 2 * n] for n in range(6))
    raw_s, raw_r, gain_s, gain_r, fac_s, fac_r, part_s, part_r, fin_s, fin_r, end_s, end_r, loc, out_sem, in_sem = scratch[27:]

    per_station, _, lanes = v.shape
    half = lanes // 2
    devices = spec[0].shape[0]
    beams_local, h = spec[0].shape[1:3]
    beams = devices * beams_local
    local = channels // devices
    stations = st_c.shape[1]
    per = h // radix
    tail = n_taps - 1
    groups = lax.axis_size("tm")
    tm = lax.axis_index("tm")
    block = ob.shape[1]
    width = channels // fsum[0].shape[0]
    me = lax.axis_index("chan")

    bar = pltpu.get_barrier_semaphore()
    a, b = sides

    def greet(time, own):
        if own:
            pl.semaphore_signal(bar, inc=1, device_id={"tm": time, "chan": me})
        for off in range(1, a.slots):
            pl.semaphore_signal(bar, inc=1, device_id={"tm": time, "chan": a.peer(off)[1]})
        for off in range(b.cores, b.slots):
            pl.semaphore_signal(bar, inc=1, device_id={"tm": time, "chan": b.peer(off)[1]})

    friends = a.slots - 1 + b.slots - b.cores
    greet(tm, False)

    @pl.when(tm > 0)
    def _():
        greet(tm - 1, True)

    @pl.when(tm < groups - 1)
    def _():
        pl.semaphore_wait(bar, 2 * friends + 1)

    @pl.when(tm == groups - 1)
    def _():
        pl.semaphore_wait(bar, friends)

    def raw_copy(side, u, off):
        s = side.which
        e, r, k = side.place()
        _, device, e2, k2 = side.peer(off)
        start = pl.multiple_of(side.device(e2, u, k2) * local + s * h, h)
        return pltpu.make_async_remote_copy(
            v.at[:, pl.ds(start, h), :],
            raw[s].at[u, e * side.cores + k],
            raw_s.at[s, u, off],
            raw_r.at[s, u, off],
            device_id={"chan": device},
        )

    def gain_copy(side, d):
        s = side.which
        e, r, k = side.place()
        r2 = (r + d) % side.reduce
        return pltpu.make_async_remote_copy(
            gains[s].at[r2],
            gbuf[s].at[r],
            gain_s.at[s, d],
            gain_r.at[s, d],
            device_id={"chan": side.device(e, r2, k)},
        )

    def factor_copy(side, off):
        s = side.which
        e, r, k = side.place()
        return pltpu.make_async_remote_copy(
            factors[s],
            fbuf[s].at[e * side.cores + k],
            fac_s.at[s, off],
            fac_r.at[s, off],
            device_id={"chan": side.peer(off)[1]},
        )

    def part_copy(side, u, d):
        s = side.which
        e, r, k = side.place()
        r2 = (r + d) % side.reduce
        return pltpu.make_async_remote_copy(
            part[s].at[u, r2],
            got[s].at[u, r],
            part_s.at[s, u, d],
            part_r.at[s, u, d],
            device_id={"chan": side.device(e, r2, k)},
        )

    def final_copy(side, u, off):
        s = side.which
        e, r, k = side.place()
        q, device, _, _ = side.peer(off)
        return pltpu.make_async_remote_copy(
            done[s].at[u, q],
            spec[s].at[side.device(e, u, k)],
            fin_s.at[s, u, off],
            fin_r.at[s, u, off],
            device_id={"chan": device},
        )

    def end_copy(side, u, off):
        s = side.which
        e, r, k = side.place()
        q, device, _, _ = side.peer(off)
        return pltpu.make_async_remote_copy(
            ends[s].at[u, q],
            halo[s].at[side.device(e, u, k)],
            end_s.at[s, u, off],
            end_r.at[s, u, off],
            device_id={"tm": jnp.minimum(tm + 1, groups - 1), "chan": device},
        )

    for side in sides:
        for off in range(1, side.slots):
            factor_copy(side, off).start()
        for d in range(1, side.reduce):
            gain_copy(side, d).start()
    for u in range(max(side.reduce for side in sides)):
        for side in sides:
            if u < side.reduce:
                for off in range(side.cores, side.slots):
                    raw_copy(side, u, off).start()
                for off in range(1, side.cores):
                    raw_copy(side, u, off).start()

    for side in sides:
        s = side.which
        e, r, k = side.place()
        copies = [
            pltpu.make_async_copy(gains[s].at[r], gbuf[s].at[r], loc.at[0]),
            pltpu.make_async_copy(factors[s], fbuf[s].at[e * side.cores + k], loc.at[1]),
            pltpu.make_async_copy(delays[s], dv[s], loc.at[2]),
        ]
        for copy in copies:
            copy.start()
        for copy in copies:
            copy.wait()

        def rotate(n, carry, s=s):
            at = pl.ds(pl.multiple_of(n * 16, 16), 16)
            angle = (TWO_PI / channels) * dv[s][at, :]
            rot_c[s][at, :] = jnp.cos(angle)
            rot_s[s][at, :] = jnp.sin(angle)
            return carry

        lax.fori_loop(0, beams // 16, rotate, 0)
    zero[...] = jnp.zeros_like(zero)

    @pl.when(tm == 0)
    def _():
        for s in range(SETS):
            for d in range(devices):
                pltpu.make_async_copy(zero, halo[s].at[d], loc.at[0]).start()
                pltpu.make_async_copy(zero, halo[s].at[d], loc.at[0]).wait()

    for side in sides:
        s = side.which
        for off in range(1, side.slots):
            factor_copy(side, off).wait_recv()
        for d in range(1, side.reduce):
            gain_copy(side, d).wait_recv()
        total = fbuf[s][0]
        for q in range(1, side.slots):
            total = total + fbuf[s][q]
        fsum[s][...] = total

    def form(side, u):
        s = side.which
        e, r, k = side.place()
        first = side.device(e, u, k) * local + s * h
        loads = []
        for off in range(side.slots):
            q = side.peer(off)[0]
            if off == 0:
                source = v.at[:, pl.ds(pl.multiple_of(first, h), h), :]
            else:
                raw_copy(side, u, off).wait_recv()
                source = raw[s].at[u, q]
            loads.append(pltpu.make_async_copy(source, xv.at[pl.ds(q * per_station, per_station)], in_sem.at[off]))
            loads[-1].start()

        turns = TWO_PI * ((first.astype(jnp.float32) + 0.5) / channels - 0.5)

        def begin(n, carry):
            at = pl.ds(pl.multiple_of(n * 16, 16), 16)
            angle = turns * dv[s][at, :]
            st_c[at, :] = jnp.cos(angle)
            st_s[at, :] = jnp.sin(angle)
            return carry

        lax.fori_loop(0, beams // 16, begin, 0)
        for load in loads:
            load.wait()

        def tile(t, carry):
            def spread(n, carry):
                x = xv[pl.ds(pl.multiple_of(n * 16, 16), 16), pl.ds(pl.multiple_of(t * 16, 16), 16), :]
                x = x.astype(jnp.float32).reshape(256, lanes)
                at = pl.ds(pl.multiple_of(n * 256, 256), 256)
                xf_re[at, :] = x[:, :half]
                xf_im[at, :] = x[:, half:]
                return carry

            lax.fori_loop(0, stations // 16, spread, 0)

            def quad(g, carry):
                c0 = t * 16 + g * QUAD
                rows = []
                for q in range(QUAD):
                    scale = fsum[s][pl.ds((first + c0 + q) // width, 1), :]
                    rows.append((gbuf[s][u, 0, pl.ds(c0 + q, 1), :] * scale, gbuf[s][u, 1, pl.ds(c0 + q, 1), :] * scale))

                def weigh(n, carry):
                    at = pl.ds(pl.multiple_of(n * 16, 16), 16)
                    c, d = st_c[at, :], st_s[at, :]
                    rc, rs = rot_c[s][at, :], rot_s[s][at, :]
                    for q in range(QUAD):
                        gr, gi = rows[q]
                        w_re[q, at, :] = (gr * c + gi * d).astype(jnp.bfloat16)
                        w_im[q, at, :] = (gi * c - gr * d).astype(jnp.bfloat16)
                        c, d = c * rc - d * rs, d * rc + c * rs
                    st_c[at, :], st_s[at, :] = c, d
                    return carry

                lax.fori_loop(0, beams // 16, weigh, 0)
                for q in range(QUAD):
                    from_rows = pl.ds(g * QUAD + q, stations, stride=16)
                    x = jnp.concatenate([xf_re[from_rows, :], xf_im[from_rows, :]], axis=1).astype(jnp.bfloat16)
                    real = jnp.dot(w_re[q], x, preferred_element_type=jnp.float32)
                    imag = jnp.dot(w_im[q], x, preferred_element_type=jnp.float32)
                    c = c0 + q
                    to_rows = pl.ds(c % radix * per + c // radix, beams, stride=h)
                    s_re[to_rows, :] = real[:, :half] - imag[:, half:]
                    s_im[to_rows, :] = real[:, half:] + imag[:, :half]
                return carry

            lax.fori_loop(0, 16 // QUAD, quad, 0)
            return carry

        lax.fori_loop(0, h // 16, tile, 0)

        held = side.slots * beams_local

        def put(n):
            to = part[s].at[u, n * block // held, pl.ds(n * block % held, block)]
            return pltpu.make_async_copy(ob.at[n % 2], to, out_sem.at[n % 2])

        def flush(n, carry):
            @pl.when(n >= 2)
            def _():
                put(n - 2).wait()

            at = pl.ds(pl.multiple_of(n * block * h, block * h), block * h)
            ob[n % 2, :, :, :half] = s_re[at, :].reshape(block, h, half).astype(ob.dtype)
            ob[n % 2, :, :, half:] = s_im[at, :].reshape(block, h, half).astype(ob.dtype)
            put(n).start()
            return carry

        lax.fori_loop(0, beams // block, flush, 0)
        for n in range(2):
            put(beams // block - 2 + n).wait()
        for d in range(1, side.reduce):
            part_copy(side, u, d).start()

    def settle(side, u):
        s = side.which
        e, r, k = side.place()
        slot = side.device(e, u, k)
        per_slot = beams_local // block
        lane = lax.broadcasted_iota(jnp.int32, (h, half), 1)
        for d in range(1, side.reduce):
            part_copy(side, u, d).wait_recv()

        def finish(off, own):
            q = side.peer(off)[0]

            def fetch(n):
                at = pl.ds(q * beams_local + n * block, block)
                copies = [pltpu.make_async_copy(part[s].at[u, r, at], pa.at[n % 2, 0], in_sem.at[n % 2 * side.reduce])]
                for d in range(1, side.reduce):
                    other = got[s].at[u, (r + d) % side.reduce, at]
                    copies.append(pltpu.make_async_copy(other, pa.at[n % 2, d], in_sem.at[n % 2 * side.reduce + d]))
                return copies

            def put(n):
                at = pl.ds(n * block, block)
                to = spec[s].at[slot, at] if own else done[s].at[u, q, at]
                return pltpu.make_async_copy(pb.at[n % 2], to, out_sem.at[n % 2])

            for copy in fetch(0):
                copy.start()
            hal[...] = jnp.zeros_like(hal)
            for n in range(per_slot):
                for copy in fetch(n):
                    copy.wait()
                if n + 1 < per_slot:
                    for copy in fetch(n + 1):
                        copy.start()
                if n >= 2:
                    put(n - 2).wait()

                def add(t, carry, n=n):
                    total = pa[n % 2, 0, t].astype(jnp.float32)
                    for d in range(1, side.reduce):
                        total = total + pa[n % 2, d, t].astype(jnp.float32)
                    pb[n % 2, t] = total.astype(pb.dtype)
                    first = n_taps * (n * block + t)
                    place = lane - first
                    keep = jnp.logical_and(place >= 0, place < tail)
                    for p in range(2):
                        cols = slice(p * half, (p + 1) * half)
                        moved = pltpu.roll(total[:, cols], (first + tail) % half, 1)
                        hal[:, cols] = jnp.where(keep, moved, hal[:, cols])
                    return carry

                lax.fori_loop(0, block, add, 0)
                put(n).start()
            for n in range(max(0, per_slot - 2), per_slot):
                put(n).wait()
            if not own:
                final_copy(side, u, off).start()

            @pl.when(tm < groups - 1)
            def _():
                hb[...] = hal[...].astype(hb.dtype)
                out = pltpu.make_async_copy(hb, ends[s].at[u, q], loc.at[1])
                out.start()
                out.wait()
                end_copy(side, u, off).start()

        def others(off, carry):
            finish(off, False)
            return carry

        lax.fori_loop(1, side.slots, others, 0)
        finish(0, True)

    def each(work):
        for u in range(max(side.reduce for side in sides)):
            for side in sides:
                if u < side.reduce:
                    work(side, u)

    def looped(work):
        if a.reduce != b.reduce:
            return each(work)

        def body(u, carry):
            for side in sides:
                work(side, u)
            return carry

        lax.fori_loop(0, a.reduce, body, 0)

    looped(form)
    looped(settle)

    for side in sides:
        for off in range(1, side.slots):
            factor_copy(side, off).wait_send()
        for d in range(1, side.reduce):
            gain_copy(side, d).wait_send()
        for u in range(side.reduce):
            for off in range(1, side.slots):
                raw_copy(side, u, off).wait_send()
                final_copy(side, u, off).wait()
            for d in range(1, side.reduce):
                part_copy(side, u, d).wait_send()

            @pl.when(tm < groups - 1)
            def _():
                for off in range(side.slots):
                    end_copy(side, u, off).wait_send()

            @pl.when(tm > 0)
            def _():
                for off in range(side.slots):
                    end_copy(side, u, off).wait_recv()


def exchange(voltages, gains, factors, delays, grid, devices, channels, radix, n_taps):
    per_station, _, lanes = voltages.shape
    half = lanes // 2
    sides = [Side(s, grid) for s in range(SETS)]
    beams = delays[0].shape[0]
    stations = delays[0].shape[1]
    beams_local = beams // devices
    h = channels // devices // SETS
    block = min(16, beams_local)
    most = max(side.slots for side in sides)
    deep = max(side.reduce for side in sides)
    bf, f32 = jnp.bfloat16, jnp.float32
    hbm = lambda *shape: jax.ShapeDtypeStruct(shape, bf)
    outs = [hbm(devices, beams_local, h, lanes)] * 2 + [hbm(devices, h, lanes)] * 2
    outs += [hbm(side.reduce, side.slots, per_station, h, lanes) for side in sides]
    outs += [hbm(side.reduce, side.reduce, side.slots * beams_local, h, lanes) for side in sides] * 2
    outs += [hbm(side.reduce, side.slots, beams_local, h, lanes) for side in sides]
    outs += [hbm(side.reduce, side.slots, h, lanes) for side in sides]
    any_space = pl.BlockSpec(memory_space=pl.ANY)
    vm = pltpu.VMEM
    blocks = factors[0].shape[0]
    scratch = [
        vm((stations, h, lanes), bf),
        vm((stations * 16, half), f32),
        vm((stations * 16, half), f32),
        vm((QUAD, beams, stations), bf),
        vm((QUAD, beams, stations), bf),
        vm((beams, stations), f32),
        vm((beams, stations), f32),
        vm((beams * h, half), f32),
        vm((beams * h, half), f32),
        vm((2, block, h, lanes), bf),
        vm((2, deep, block, h, lanes), bf),
        vm((2, block, h, lanes), bf),
        vm((h, lanes), f32),
        vm((h, lanes), bf),
        vm((h, lanes), bf),
    ]
    scratch += [vm((side.reduce, 2, h, stations), f32) for side in sides]
    scratch += [vm((side.slots, blocks, stations), f32) for side in sides]
    scratch += [vm((blocks, stations), f32) for _ in sides]
    scratch += [vm((beams, stations), f32)] * 6
    dma = pltpu.SemaphoreType.DMA
    scratch += [dma((SETS, deep, most))] * 2 + [dma((SETS, deep))] * 2 + [dma((SETS, most))] * 2
    scratch += [dma((SETS, deep, deep))] * 2 + [dma((SETS, deep, most))] * 4
    scratch += [dma((3,)), dma((2,)), dma((max(most, 2 * deep),))]
    results = pl.pallas_call(
        functools.partial(exchange_kernel, grid, n_taps, channels, radix),
        name="exchange",
        in_specs=[any_space] * 7,
        out_specs=[any_space] * len(outs),
        out_shape=outs,
        scratch_shapes=scratch,
        compiler_params=pltpu.CompilerParams(
            collective_id=0, has_side_effects=True, vmem_limit_bytes=VMEM_LIMIT
        ),
    )(voltages, *gains, *factors, *delays)
    return results[:2], results[2:4]


def times_unit(value, turn, radix):
    re, im = value
    quarter = turn * (4 // radix) % 4
    return ((re, im), (-im, re), (-re, -im), (im, -re))[quarter]


def combine(values, q):
    radix = len(values)
    re, im = values[0]
    for r in range(1, radix):
        more_re, more_im = times_unit(values[r], r * q, radix)
        re, im = re + more_re, im + more_im
    return re, im


def synthesis_kernel(radix, *refs):
    tab, taps_masked = refs[:2]
    blocks = refs[2 : 2 + SETS]
    halos = refs[2 + SETS : 2 + 2 * SETS]
    o, partial, before = refs[2 + 2 * SETS :]
    n_taps, channels, half = taps_masked.shape
    span = channels // radix
    rows = 16
    beam = pl.program_id(0)

    def transform(chunks, slot, r):
        per = chunks[0].shape[1] // radix
        parts = [c[:, r * per : (r + 1) * per, :].reshape(-1, 2 * half) for c in chunks]
        x = jnp.concatenate(parts, axis=0)
        turned = jnp.concatenate([-x[:, half:], x[:, :half]], axis=1)
        both = jnp.concatenate([x, turned], axis=0)
        partial[slot, r] = jnp.dot(tab[r], both, preferred_element_type=jnp.float32)

    def on_rows(start, slot, store):
        values = []
        for r in range(radix):
            both = partial[slot, r, pl.ds(start, rows), :]
            values.append((both[:, :half], both[:, half:]))
        for q in range(radix):
            store(pl.ds(q * span + start, rows), combine(values, q))

    lane = lax.broadcasted_iota(jnp.int32, (rows, half), 1)

    @pl.when(beam == 0)
    def _():
        for r in range(radix):
            transform(halos, 1, r)
        frame = lane % n_taps

        def store(at, signal):
            for part in range(2):
                total = jnp.zeros((rows, half), jnp.float32)
                for k in range(1, n_taps):
                    back = n_taps - 1 - k
                    moved = pltpu.roll(signal[part], (half - back) % half, 1) if back else signal[part]
                    tap = jnp.broadcast_to(taps_masked[k, at, :][:, half - 1 :], (rows, half))
                    total = total + jnp.where(frame < k, tap * moved, 0.0)
                before[at, part * half : (part + 1) * half] = total

        def body(i, carry):
            on_rows(pl.multiple_of(i * rows, rows), 1, store)
            return carry

        lax.fori_loop(0, span // rows, body, 0)

    new, old = beam % 2, (beam + 1) % 2
    shift = (half - n_taps * jnp.maximum(beam - 1, 0)) % half

    def store(at, signal):
        for part in range(2):
            cols = slice(part * half, (part + 1) * half)
            total = taps_masked[0, at, :] * signal[part]
            for k in range(1, n_taps):
                total = total + taps_masked[k, at, :] * pltpu.roll(signal[part], k, 1)
            total = total + jnp.where(lane < n_taps - 1, pltpu.roll(before[at, cols], shift, 1), 0.0)
            o[at, cols] = total.astype(o.dtype)

    for r in range(radix):
        transform(blocks, new, r)
        for start in range(r * span // radix, (r + 1) * span // radix, rows):
            on_rows(start, old, store)


def synthesize(tables, filter_taps, spectra, halos, radix):
    devices, beams, chunk_channels, lanes = spectra[0].shape
    n_taps, channels = filter_taps.shape
    half = lanes // 2
    span = channels // radix
    with jax.named_scope("taps"):
        taps = jnp.broadcast_to(filter_taps[:, :, None], (n_taps, channels, half))
        lane = lax.broadcasted_iota(jnp.int32, taps.shape, 2)
        masked = jnp.where(lane >= lax.broadcasted_iota(jnp.int32, taps.shape, 0), taps, 0.0)
    whole = lambda shape: pl.BlockSpec(shape, lambda b: (0,) * len(shape), pipeline_mode=pl.Buffered(1))
    return pl.pallas_call(
        functools.partial(synthesis_kernel, radix),
        name="synthesize",
        grid=(beams + 1,),
        in_specs=[whole(tables.shape), whole(taps.shape)]
        + [pl.BlockSpec((devices, None, chunk_channels, lanes), lambda b: (0, jnp.minimum(b, beams - 1), 0, 0))] * SETS
        + [whole(halos[0].shape)] * SETS,
        out_specs=pl.BlockSpec((None, channels, lanes), lambda b: (jnp.maximum(b - 1, 0), 0, 0)),
        out_shape=jax.ShapeDtypeStruct((beams, channels, lanes), jnp.bfloat16),
        scratch_shapes=[
            pltpu.VMEM((2, radix, span, lanes), jnp.float32),
            pltpu.VMEM((channels, lanes), jnp.float32),
        ],
        compiler_params=pltpu.CompilerParams(vmem_limit_bytes=56 * 1024 * 1024),
    )(tables, masked, *spectra, *halos)


def per_device(voltages, exponents, gain_real, gain_imag, delays, filter_taps):
    per_station, channels, lanes = voltages.shape
    devices = lax.axis_size("chan")
    local = channels // devices
    h = local // SETS
    radix = radix_of(h)
    beams = delays.shape[1]
    beams_local = beams // devices
    n_taps = filter_taps.shape[0]
    grid = chip_grid(devices)
    rows, cols, cores = grid
    n_stations = delays.shape[0]
    normalizer = 1.0 / math.sqrt(n_stations)
    factor = jnp.exp2(exponents[:, :, 0].astype(jnp.float32)).astype(jnp.bfloat16).astype(jnp.float32)
    gains, factors, angles = [], [], []
    for s in range(SETS):
        side = Side(s, grid)
        e, r, k = side.place()
        with jax.named_scope(f"prepare_{s}"):
            pair = []
            for gain in (gain_real, gain_imag):
                part = (gain[:, s * h : (s + 1) * h] * normalizer).reshape(rows, cols, cores * per_station, h)
                order = (1, 3, 0, 2) if s == 0 else (0, 3, 1, 2)
                pair.append(jnp.transpose(part, order).reshape(side.reduce, h, -1))
            gains.append(jnp.stack(pair, axis=1))
            here = lax.broadcasted_iota(jnp.int32, (1, side.slots, 1), 1) == e * cores + k
            placed = jnp.where(here, jnp.transpose(factor)[:, None, :], 0.0)
            factors.append(placed.reshape(factor.shape[1], side.slots * per_station))
            table = delays.reshape(rows, cols, cores * per_station, rows, cols, cores * beams_local)
            table = lax.dynamic_index_in_dim(table, r, 1 - s, keepdims=False)
            order = (3, 2, 4, 0, 1) if s == 0 else (2, 3, 4, 0, 1)
            angles.append(jnp.transpose(table, order).reshape(beams, side.slots * per_station))
    with jax.named_scope("exchange"):
        spectra, halos = exchange(voltages, gains, factors, angles, grid, devices, channels, radix, n_taps)
    with jax.named_scope("tables"):
        tables = synthesis_tables(channels, devices, h, radix)
    return synthesize(tables, filter_taps, spectra, halos, radix)


def solution(mesh):
    placed = (
        P("chan", None, "tm"),
        P("chan", None, "tm"),
        P(None, "chan"),
        P(None, "chan"),
        P(),
        P(),
    )
    return jax.shard_map(per_device, mesh=mesh, in_specs=placed, out_specs=P("chan", None, "tm"), check_vma=False)
```

profile of v0, /device:TPU:17, one launch (start us, length us, event | category | flops | bytes accessed | tf_op | source)
XLA Modules:
  0.0 539.2 jit_solution(10123566133770952543)
XLA Ops:
  0.0 1.2 copy.22
  1.2 0.3 reshape.65
  1.6 0.3 constant_dynamic-slice_fusion.1
  1.9 0.2 copy.24
  2.1 0.1 constant_dynamic-slice_fusion
  2.2 0.8 copy_bitcast_fusion
  3.1 0.1 broadcast_in_dim.59
  3.2 0.1 broadcast_in_dim.60
  3.3 0.1 broadcast_in_dim.53
  3.3 0.1 broadcast_in_dim.54
  3.4 0.7 convert_convert_fusion
  4.2 0.1 broadcast_in_dim.57
  4.2 0.6 broadcast_select_fusion
  4.9 1.2 slice_multiply_fusion.1
  6.1 0.1 copy.18
  6.2 0.1 reshape.58
  6.3 1.2 slice_multiply_fusion
  7.5 0.1 copy.19
  7.6 0.1 reshape.60
  7.7 0.1 copy.20
  7.9 0.1 reshape.62
  8.0 0.1 copy.21
  8.1 0.1 reshape.64
  8.2 0.8 pad_maximum_fusion.1
  9.1 0.0 copy-start
  9.1 464.3 %exchange.1 = (bf16[8,32,64,256]{3,2,1,0:T(8,128)(2,1)}, bf16[8,32,64,256]{3,2,1,0:T(8,128)(2,1)}, bf16[8,64,256]{2,1,0:T(8,128)(2,1)}, bf16[8,64,256]{2,1,0:T(8...) custom-call(bf16[64,1024,256]{2,1,0:T(8,128)(2,1)} %refs_0_.1, ...), custom_call_target="tpu_custom_call" | custom-call | tf_op jit(solution)/shard_map/exchange/exchange/pallas_call | solution.py:509
  473.4 4.4 multiply_convert_fusion.1
  477.8 1.1 pad_maximum_fusion.refs_0_
  478.9 0.0 copy-done
  478.9 1.9 fusion.refs_1_
  480.8 58.4 %synthesize.1 = bf16[32,1024,256]{2,1,0:T(8,128)(2,1)} custom-call(bf16[4,256,512]{2,1,0:T(8,128)(2,1)} %pad_maximum_fusion.refs_0_, f32[4,1024,128]{2,1,0:T(8,128)} %fusion.refs_1_, bf16[8,32,64,256]{3,2,1,0:T(8,128)(2,1)} %get-tuple-element.9.refs_2_, bf16[8,32,64,256]{3,2,1,0:T(8,128)(2,1)} %get-tuple-element.10.refs_3_, ...), custom_call_target="tpu_custom_call" | custom-call | tf_op jit(solution)/shard_map/synthesize/pallas_call | solution.py:616
  (9 shorter events, 0.1 us)
Async XLA Ops:
  9.1 469.8 %copy-start = (f32[4,1024]{1,0:T(4,128)S(1)}, f32[4,1024]{1,0:T(4,128)}, u32[]{:S(2)}) copy-start(f32[4,1024]{1,0:T(4,128)} %param.11) | copy-start | bytes 49156
where the time goes:
time: 540 us; the launch traced here: 539 us
  Pallas kernels  523 us (97%)
  other arithmetic  12 us (2%)
    pallas_call x1, Pallas kernels, exchange(): pl.pallas_call(functools.partial(exchange_kernel, grid, n_taps, channels,...  464 us
    pallas_call x1, Pallas kernels, synthesize(): pl.pallas_call(functools.partial(synthesis_kernel, radix), name='synthesi...  58.4 us

commit v1 on v0

v1 whole, which is shorter than its diff:
```python
import functools
import math

import jax
import jax.numpy as jnp
from jax import lax
from jax.experimental import pallas as pl
from jax.experimental.pallas import tpu as pltpu
import numpy as np
from jax.sharding import PartitionSpec as P

TWO_PI = 6.283185307179586
SETS = 2
QUAD = 4
VMEM_LIMIT = 60 * 1024 * 1024


def radix_of(chunk_channels):
    return max(r for r in (4, 2, 1) if chunk_channels % r == 0 and (chunk_channels // r) % 16 == 0 or r == 1)


def chip_grid(devices):
    cores = 2 if devices % 2 == 0 else 1
    chips = devices // cores
    rows = max(r for r in range(1, chips + 1) if chips % r == 0 and r * r <= chips)
    return rows, chips // rows, cores


class Side:
    def __init__(self, which, grid):
        self.rows, self.cols, self.cores = grid
        self.which = which
        self.group, self.reduce = (self.rows, self.cols) if which == 0 else (self.cols, self.rows)
        self.slots = self.group * self.cores

    def device(self, e, r, k):
        i, j = (e, r) if self.which == 0 else (r, e)
        return (i * self.cols + j) * self.cores + k

    def place(self):
        d = lax.axis_index("chan")
        k = d % self.cores
        j = d // self.cores % self.cols
        i = d // (self.cores * self.cols)
        return (i, j, k) if self.which == 0 else (j, i, k)

    def peer(self, off):
        e, r, k = self.place()
        e2 = (e + off // self.cores) % self.group
        k2 = (k + off % self.cores) % self.cores
        return e2 * self.cores + k2, self.device(e2, r, k2), e2, k2


def exchange_kernel(grid, n_taps, channels, radix, *refs):
    sides = [Side(s, grid) for s in range(SETS)]
    v, factors, gains, dl, ft, base = refs[0], refs[1:3], refs[3:5], refs[5], refs[6], refs[7]
    out = refs[8]
    spec, raw, part, got, done = (refs[9 + 2 * n : 11 + 2 * n] for n in range(5))
    scratch = refs[19:]
    xv, xf_re, xf_im, w_re, w_im, st_c, st_s, s_re, s_im, ob = scratch[:10]
    tab, taps, partial, before, xin, oo, ftv, basev = scratch[10:18]
    pa, pb = scratch[18:20]
    pairs = (scratch[20 + 2 * n : 22 + 2 * n] for n in range(12))
    gt, gsel, gbuf, fbuf, fsum, dtmp, dv, rot_c, rot_s, hal, hb, hv = pairs
    sems = scratch[44:]
    raw_s, raw_r, gain_s, gain_r, fac_s, fac_r, part_s, part_r, fin_s, fin_r, end_s, end_r = sems[:12]
    gain_in, delay_in, extra_in, own_in, load_in, out_sem, fetch_in, put_sem, x_in, o_out = sems[12:]

    per_station, _, lanes = v.shape
    half = lanes // 2
    beams_local = spec[0].shape[1]
    devices, h = spec[0].shape[0], spec[0].shape[2]
    beams = devices * beams_local
    local = channels // devices
    stations = st_c.shape[1]
    per = h // radix
    span = channels // radix
    tail = n_taps - 1
    groups = lax.axis_size("tm")
    tm = lax.axis_index("tm")
    block = ob.shape[1]
    piece = beams_local // fin_s.shape[3]
    pieces = beams_local // piece
    early = max(1, 5 * pieces // 8)
    width = channels // fsum[0].shape[0]
    me = lax.axis_index("chan")
    rows, cols, cores = grid
    normalizer = 1.0 / math.sqrt(rows * cols * cores * per_station)

    bar = pltpu.get_barrier_semaphore()
    a, b = sides

    def greet(time, own):
        if own:
            pl.semaphore_signal(bar, inc=1, device_id={"tm": time, "chan": me})
        for off in range(1, a.slots):
            pl.semaphore_signal(bar, inc=1, device_id={"tm": time, "chan": a.peer(off)[1]})
        for off in range(b.cores, b.slots):
            pl.semaphore_signal(bar, inc=1, device_id={"tm": time, "chan": b.peer(off)[1]})

    friends = a.slots - 1 + b.slots - b.cores
    greet(tm, False)

    @pl.when(tm > 0)
    def _():
        greet(tm - 1, True)

    @pl.when(tm < groups - 1)
    def _():
        pl.semaphore_wait(bar, 2 * friends + 1)

    @pl.when(tm == groups - 1)
    def _():
        pl.semaphore_wait(bar, friends)

    def raw_copy(side, u, off):
        s = side.which
        e, r, k = side.place()
        _, device, e2, k2 = side.peer(off)
        start = pl.multiple_of(side.device(e2, u, k2) * local + s * h, h)
        return pltpu.make_async_remote_copy(
            v.at[:, pl.ds(start, h), :],
            raw[s].at[u, e * side.cores + k],
            raw_s.at[s, u, off],
            raw_r.at[s, u, off],
            device_id={"chan": device},
        )

    def gain_copy(side, d):
        s = side.which
        e, r, k = side.place()
        r2 = (r + d) % side.reduce
        return pltpu.make_async_remote_copy(
            gsel[s].at[r2],
            gbuf[s].at[r],
            gain_s.at[s, d],
            gain_r.at[s, d],
            device_id={"chan": side.device(e, r2, k)},
        )

    def factor_copy(side, off):
        s = side.which
        e, r, k = side.place()
        return pltpu.make_async_remote_copy(
            factors[s],
            fbuf[s].at[e * side.cores + k],
            fac_s.at[s, off],
            fac_r.at[s, off],
            device_id={"chan": side.peer(off)[1]},
        )

    def part_copy(side, u, d):
        s = side.which
        e, r, k = side.place()
        r2 = (r + d) % side.reduce
        return pltpu.make_async_remote_copy(
            part[s].at[u, r2],
            got[s].at[u, r],
            part_s.at[s, u, d],
            part_r.at[s, u, d],
            device_id={"chan": side.device(e, r2, k)},
        )

    def final_copy(side, u, off, g):
        s = side.which
        e, r, k = side.place()
        q, device, _, _ = side.peer(off)
        at = pl.ds(g * piece, piece)
        return pltpu.make_async_remote_copy(
            done[s].at[u, q, at],
            spec[s].at[side.device(e, u, k), at],
            fin_s.at[s, u, off, g],
            fin_r.at[s, u, off, g],
            device_id={"chan": device},
        )

    def end_copy(side, u, off):
        s = side.which
        e, r, k = side.place()
        q, device, _, _ = side.peer(off)
        return pltpu.make_async_remote_copy(
            hb[s].at[u, q],
            hv[s].at[side.device(e, u, k)],
            end_s.at[s, u, off],
            end_r.at[s, u, off],
            device_id={"tm": jnp.minimum(tm + 1, groups - 1), "chan": device},
        )

    def span_of(side, source, r):
        return source.at[:, r] if side.which == 0 else source.at[r]

    def start_raw(u):
        for side in sides:
            if u < side.reduce:
                for off in range(side.cores, side.slots):
                    raw_copy(side, u, off).start()
                for off in range(1, side.cores):
                    raw_copy(side, u, off).start()

    def loop(low, high, work):
        def body(n, carry):
            work(n)
            return carry

        lax.fori_loop(low, high, body, 0)

    def aligned(n, size):
        return pl.ds(pl.multiple_of(n * size, size), size)

    start_raw(0)
    gain_loads, delay_loads, extra_loads, own_loads = [], [], [], []
    for side in sides:
        s = side.which
        e, r, k = side.place()
        for off in range(1, side.slots):
            factor_copy(side, off).start()
        for r2 in range(side.reduce):
            for p in range(2):
                source = span_of(side, gains[p], r2)
                gain_loads.append(pltpu.make_async_copy(source, gt[s].at[r2, p], gain_in.at[s, r2, p]))
        delay_loads.append(pltpu.make_async_copy(span_of(side, dl, r), dtmp[s], delay_in.at[s]))
        own_loads.append(pltpu.make_async_copy(factors[s], fbuf[s].at[e * side.cores + k], own_in.at[s]))
    extra_loads = [pltpu.make_async_copy(ft, ftv, extra_in.at[0]), pltpu.make_async_copy(base, basev, extra_in.at[1])]
    loads = gain_loads + delay_loads + own_loads + extra_loads
    for load in loads:
        load.start()
    for load in loads:
        load.wait()
    for side in sides:
        s = side.which
        for r2 in range(side.reduce):
            for p in range(2):
                turned = jnp.transpose(gt[s][r2, p].reshape(stations, local))
                gsel[s][r2, p] = turned[s * h : (s + 1) * h] * normalizer
    for side in sides:
        s = side.which
        turned = jnp.transpose(dtmp[s][...].reshape(stations, beams))
        held = cores * beams_local
        for i in range(rows):
            for j in range(cols):
                e, r = (i, j) if s == 0 else (j, i)
                to = (r * side.group + e) * held
                at = (i * cols + j) * held
                dv[s][to : to + held, :] = turned[at : at + held]
    for side in sides:
        for d in range(1, side.reduce):
            gain_copy(side, d).start()
    for u in range(1, max(side.reduce for side in sides)):
        start_raw(u)

    for side in sides:
        s = side.which
        r = side.place()[1]
        gbuf[s][r] = gsel[s][r]

        def rotate(n, s=s):
            at = aligned(n, 16)
            angle = (TWO_PI / channels) * dv[s][at, :]
            rot_c[s][at, :] = jnp.cos(angle)
            rot_s[s][at, :] = jnp.sin(angle)

        loop(0, beams // 16, rotate)
    for r in range(radix):

        def tabulate(n, r=r):
            at = aligned(n, 16)
            sample = n * 16 + lax.broadcasted_iota(jnp.int32, (16, span), 0)
            product = sample * (basev[0:1, :] + r)
            product = product & (channels - 1) if channels & (channels - 1) == 0 else lax.rem(product, channels)
            phases = TWO_PI / channels * product.astype(jnp.float32)
            tab[r, at, :span] = (jnp.cos(phases) * (1.0 / math.sqrt(channels))).astype(tab.dtype)
            tab[r, at, span:] = (jnp.sin(phases) * (1.0 / math.sqrt(channels))).astype(tab.dtype)

        loop(0, span // 16, tabulate)

    def spread_taps(n):
        at = aligned(n, half)
        lane = lax.broadcasted_iota(jnp.int32, (half, half), 1)
        for k in range(n_taps):
            column = jnp.transpose(jnp.broadcast_to(ftv[k : k + 1, at], (half, half)))
            taps[k, at, :] = jnp.where(lane >= k, column, 0.0)

    loop(0, channels // half, spread_taps)
    for side in sides:
        s = side.which
        hal[s][...] = jnp.zeros_like(hal[s])
        for off in range(1, side.slots):
            factor_copy(side, off).wait_recv()
        for d in range(1, side.reduce):
            gain_copy(side, d).wait_recv()
        total = fbuf[s][0]
        for q in range(1, side.slots):
            total = total + fbuf[s][q]
        fsum[s][...] = total

    @pl.when(tm == 0)
    def _():
        for s in range(SETS):
            hv[s][...] = jnp.zeros_like(hv[s])

    def form(side, u):
        s = side.which
        e, r, k = side.place()
        first = side.device(e, u, k) * local + s * h
        loads = []
        for off in range(side.slots):
            q = side.peer(off)[0]
            if off == 0:
                source = v.at[:, pl.ds(pl.multiple_of(first, h), h), :]
            else:
                raw_copy(side, u, off).wait_recv()
                source = raw[s].at[u, q]
            loads.append(pltpu.make_async_copy(source, xv.at[pl.ds(q * per_station, per_station)], load_in.at[off]))
            loads[-1].start()

        turns = TWO_PI * ((first.astype(jnp.float32) + 0.5) / channels - 0.5)

        def begin(n):
            at = aligned(n, 16)
            angle = turns * dv[s][at, :]
            st_c[at, :] = jnp.cos(angle)
            st_s[at, :] = jnp.sin(angle)

        loop(0, beams // 16, begin)
        for load in loads:
            load.wait()

        def tile(t):
            def spread(n):
                x = xv[aligned(n, 16), aligned(t, 16), :]
                x = x.astype(jnp.float32).reshape(256, lanes)
                at = aligned(n, 256)
                xf_re[at, :] = x[:, :half]
                xf_im[at, :] = x[:, half:]

            loop(0, stations // 16, spread)

            def quad(g):
                c0 = t * 16 + g * QUAD
                pair = []
                for q in range(QUAD):
                    scale = fsum[s][pl.ds((first + c0 + q) // width, 1), :]
                    pair.append((gbuf[s][u, 0, pl.ds(c0 + q, 1), :] * scale, gbuf[s][u, 1, pl.ds(c0 + q, 1), :] * scale))

                def weigh(n):
                    at = aligned(n, 16)
                    c, d = st_c[at, :], st_s[at, :]
                    rc, rs = rot_c[s][at, :], rot_s[s][at, :]
                    for q in range(QUAD):
                        gr, gi = pair[q]
                        w_re[q, at, :] = (gr * c + gi * d).astype(jnp.bfloat16)
                        w_im[q, at, :] = (gi * c - gr * d).astype(jnp.bfloat16)
                        c, d = c * rc - d * rs, d * rc + c * rs
                    st_c[at, :], st_s[at, :] = c, d

                loop(0, beams // 16, weigh)
                for q in range(QUAD):
                    from_rows = pl.ds(g * QUAD + q, stations, stride=16)
                    x = jnp.concatenate([xf_re[from_rows, :], xf_im[from_rows, :]], axis=1).astype(jnp.bfloat16)
                    real = jnp.dot(w_re[q], x, preferred_element_type=jnp.float32)
                    imag = jnp.dot(w_im[q], x, preferred_element_type=jnp.float32)
                    c = c0 + q
                    to_rows = pl.ds(c % radix * per + c // radix, beams, stride=h)
                    s_re[to_rows, :] = real[:, :half] - imag[:, half:]
                    s_im[to_rows, :] = real[:, half:] + imag[:, :half]

            loop(0, 16 // QUAD, quad)

        loop(0, h // 16, tile)

        held = side.slots * beams_local

        def put(n):
            to = part[s].at[u, n * block // held, pl.ds(n * block % held, block)]
            return pltpu.make_async_copy(ob.at[n % 2], to, out_sem.at[n % 2])

        def flush(n):
            @pl.when(n >= 2)
            def _():
                put(n - 2).wait()

            at = aligned(n, block * h)
            ob[n % 2, :, :, :half] = s_re[at, :].reshape(block, h, half).astype(ob.dtype)
            ob[n % 2, :, :, half:] = s_im[at, :].reshape(block, h, half).astype(ob.dtype)
            put(n).start()

        loop(0, beams // block, flush)
        for n in range(2):
            put(beams // block - 2 + n).wait()
        for d in range(1, side.reduce):
            part_copy(side, u, d).start()

    def settle(side, u, send):
        s = side.which
        e, r, k = side.place()
        slot = side.device(e, u, k)
        lane = lax.broadcasted_iota(jnp.int32, (h, half), 1)
        ahead = pa.shape[0] - 1
        count = beams_local // block * side.slots
        for d in range(1, side.reduce):
            part_copy(side, u, d).wait_recv()

        def where_of(n):
            return side.peer(n % side.slots)[0], n // side.slots

        def fetch(n):
            q, g = where_of(n)
            at = pl.ds(q * beams_local + g * block, block)
            now = n % (ahead + 1)
            copies = [pltpu.make_async_copy(part[s].at[u, r, at], pa.at[now, 0], fetch_in.at[now, 0])]
            for d in range(1, side.reduce):
                other = got[s].at[u, (r + d) % side.reduce, at]
                copies.append(pltpu.make_async_copy(other, pa.at[now, d], fetch_in.at[now, d]))
            return copies

        def put(n, own):
            q, g = where_of(n)
            at = pl.ds(g * block, block)
            to = spec[s].at[slot, at] if own else done[s].at[u, q, at]
            return pltpu.make_async_copy(pb.at[n % 2], to, put_sem.at[n % 2])

        def pass_on(n):
            put(n, False).wait()
            if send:
                for g in range(block // piece):
                    at = n // side.slots * (block // piece) + g

                    @pl.when(jnp.logical_and(n % side.slots > 0, at < early))
                    def _(at=at):
                        final_copy(side, u, n % side.slots, at).start()

        for n in range(min(ahead, count)):
            for copy in fetch(n):
                copy.start()

        def step(n):
            q, g = where_of(n)
            now = n % (ahead + 1)
            for copy in fetch(n):
                copy.wait()

            @pl.when(n + ahead < count)
            def _():
                for copy in fetch(n + ahead):
                    copy.start()

            def add(t):
                total = pa[now, 0, t].astype(jnp.float32)
                for d in range(1, side.reduce):
                    total = total + pa[now, d, t].astype(jnp.float32)
                pb[n % 2, t] = total.astype(pb.dtype)
                first = n_taps * (g * block + t)
                place = lane - first
                keep = jnp.logical_and(place >= 0, place < tail)
                for p in range(2):
                    at = slice(p * half, (p + 1) * half)
                    moved = pltpu.roll(total[:, at], (first + tail) % half, 1)
                    hal[s][u, q, :, at] = jnp.where(keep, moved, hal[s][u, q, :, at])

            def add_pair(t):
                add(2 * t)
                add(2 * t + 1)

            loop(0, block // 2, add_pair)

            @pl.when(n > 0)
            def _():
                pass_on(n - 1)

            @pl.when(n % side.slots == 0)
            def _():
                put(n, True).start()

            @pl.when(n % side.slots > 0)
            def _():
                put(n, False).start()

        loop(0, count, step)
        pass_on(count - 1)
        hb[s][u] = hal[s][u].astype(hb[s].dtype)

    def each(low, high, work):
        if a.reduce == b.reduce:

            def both(u):
                for side in sides:
                    work(side, u)

            loop(low, a.reduce + high, both)
        else:
            for side in sides:
                loop(low, side.reduce + high, functools.partial(work, side))

    each(0, 0, form)
    each(0, -1, lambda side, u: settle(side, u, True))
    for side in sides:
        settle(side, side.reduce - 1, False)

    @pl.when(tm < groups - 1)
    def _():
        for side in sides:
            for u in range(side.reduce):
                for off in range(side.slots):
                    end_copy(side, u, off).start()

    def send(side, u, g):
        for off in range(side.cores, side.slots):
            final_copy(side, u, off, g).start()
        for off in range(1, side.cores):
            final_copy(side, u, off, g).start()

    def send_last(g):
        for side in sides:
            send(side, side.reduce - 1, g)

    def send_rest(g):
        for side in sides:
            for u in range(side.reduce):
                send(side, u, g)

    loop(0, early, send_last)
    loop(early, pieces, send_rest)

    @pl.when(tm > 0)
    def _():
        for side in sides:
            for u in range(side.reduce):
                for off in range(side.slots):
                    end_copy(side, u, off).wait_recv()

    lane = lax.broadcasted_iota(jnp.int32, (16, half), 1)

    def transform(source, slot, r):
        parts = [source(s, slice(r * per, (r + 1) * per)).reshape(-1, lanes) for s in range(SETS)]
        x = jnp.concatenate(parts, axis=0)
        turned = jnp.concatenate([-x[:, half:], x[:, :half]], axis=1)
        both = jnp.concatenate([x, turned], axis=0)
        partial[slot, r] = jnp.dot(tab[r], both, preferred_element_type=jnp.float32)

    def on_rows(start, slot, store):
        values = []
        for r in range(radix):
            both = partial[slot, r, pl.ds(start, 16), :]
            values.append((both[:, :half], both[:, half:]))
        for q in range(radix):
            store(pl.ds(q * span + start, 16), combine(values, q))

    for r in range(radix):
        transform(lambda s, at: hv[s][:, at, :], 1, r)
    frame = lane % n_taps

    def keep_before(at, signal):
        for p in range(2):
            total = jnp.zeros((16, half), jnp.float32)
            for k in range(1, n_taps):
                back = n_taps - 1 - k
                moved = pltpu.roll(signal[p], (half - back) % half, 1) if back else signal[p]
                tap = jnp.broadcast_to(taps[k, at, :][:, half - 1 :], (16, half))
                total = total + jnp.where(frame < k, tap * moved, 0.0)
            before[at, p * half : (p + 1) * half] = total

    loop(0, span // 16, lambda n: on_rows(pl.multiple_of(n * 16, 16), 1, keep_before))

    def fetch_beam(n):
        return [
            pltpu.make_async_copy(spec[s].at[:, n], xin.at[n % 2, s], x_in.at[n % 2, s]) for s in range(SETS)
        ]

    def arrive(g):
        for side in sides:
            for u in range(side.reduce):
                for off in range(1, side.slots):
                    final_copy(side, u, off, g).wait_recv()

    def send_out(n):
        return pltpu.make_async_copy(oo.at[n % 2], out.at[n], o_out.at[n % 2])

    arrive(0)
    for copy in fetch_beam(0):
        copy.start()

    def synthesize(n):
        @pl.when(n < beams_local)
        def _():
            for copy in fetch_beam(n):
                copy.wait()

        more = jnp.logical_and((n + 1) % piece > 0, n + 1 < beams_local)

        @pl.when(more)
        def _():
            for copy in fetch_beam(n + 1):
                copy.start()

        @pl.when(n >= 3)
        def _():
            send_out(n - 3).wait()

        new, old = n % 2, (n + 1) % 2
        shift = (half - n_taps * jnp.maximum(n - 1, 0)) % half

        def store(at, signal):
            for p in range(2):
                cut = slice(p * half, (p + 1) * half)
                total = taps[0, at, :] * signal[p]
                for k in range(1, n_taps):
                    total = total + taps[k, at, :] * pltpu.roll(signal[p], k, 1)
                total = total + jnp.where(lane < tail, pltpu.roll(before[at, cut], shift, 1), 0.0)
                oo[old, at, cut] = total.astype(oo.dtype)

        for r in range(radix):
            transform(lambda s, at: xin[new, s, :, at, :], new, r)
            for start in range(r * span // radix, (r + 1) * span // radix, 16):
                on_rows(start, old, store)

        @pl.when(n >= 1)
        def _():
            send_out(n - 1).start()

        @pl.when(jnp.logical_and((n + 1) % piece == 0, n + 1 < beams_local))
        def _():
            arrive((n + 1) // piece)
            for copy in fetch_beam(n + 1):
                copy.start()

    loop(0, beams_local + 1, synthesize)
    for n in range(max(0, beams_local - 2), beams_local):
        send_out(n).wait()

    for side in sides:
        for off in range(1, side.slots):
            factor_copy(side, off).wait_send()
        for d in range(1, side.reduce):
            gain_copy(side, d).wait_send()

        def finish(u, side=side):
            for off in range(1, side.slots):
                raw_copy(side, u, off).wait_send()
                loop(0, pieces, lambda g: final_copy(side, u, off, g).wait_send())
            for d in range(1, side.reduce):
                part_copy(side, u, d).wait_send()

            @pl.when(tm < groups - 1)
            def _():
                for off in range(side.slots):
                    end_copy(side, u, off).wait_send()

        loop(0, side.reduce, finish)


def place_map(channels, devices, chunk_channels, radix):
    span = channels // radix
    per = chunk_channels // radix
    place = np.arange(span)
    chunk, source = place // (devices * per), place // per % devices
    channel = source * SETS * chunk_channels + chunk * chunk_channels + place % per * radix
    return jnp.asarray(np.broadcast_to(channel, (8, span)), jnp.int32)


def exchange(voltages, factors, gains, delays, filter_taps, grid, devices, beams, radix):
    per_station, channels, lanes = voltages.shape
    half = lanes // 2
    n_taps = filter_taps.shape[0]
    sides = [Side(s, grid) for s in range(SETS)]
    stations = factors[0].shape[1]
    beams_local = beams // devices
    local = channels // devices
    h = local // SETS
    span = channels // radix
    block = min(16, beams_local)
    piece = min(4, beams_local)
    most = max(side.slots for side in sides)
    deep = max(side.reduce for side in sides)
    bf, f32 = jnp.bfloat16, jnp.float32
    hbm = lambda *shape: jax.ShapeDtypeStruct(shape, bf)
    outs = [hbm(beams_local, channels, lanes)]
    outs += [hbm(devices, beams_local, h, lanes)] * 2
    outs += [hbm(side.reduce, side.slots, per_station, h, lanes) for side in sides]
    outs += [hbm(side.reduce, side.reduce, side.slots * beams_local, h, lanes) for side in sides] * 2
    outs += [hbm(side.reduce, side.slots, beams_local, h, lanes) for side in sides]
    any_space = pl.BlockSpec(memory_space=pl.ANY)
    vm = pltpu.VMEM
    blocks = factors[0].shape[0]
    base = place_map(channels, devices, h, radix)
    scratch = [
        vm((stations, h, lanes), bf),
        vm((stations * 16, half), f32),
        vm((stations * 16, half), f32),
        vm((QUAD, beams, stations), bf),
        vm((QUAD, beams, stations), bf),
        vm((beams, stations), f32),
        vm((beams, stations), f32),
        vm((beams * h, half), f32),
        vm((beams * h, half), f32),
        vm((2, block, h, lanes), bf),
        vm((radix, span, 2 * span), bf),
        vm((n_taps, channels, half), f32),
        vm((2, radix, span, lanes), f32),
        vm((channels, lanes), f32),
        vm((2, SETS, devices, h, lanes), bf),
        vm((2, channels, lanes), bf),
        vm(filter_taps.shape, f32),
        vm(base.shape, jnp.int32),
        vm((3, deep, block, h, lanes), bf),
        vm((2, block, h, lanes), bf),
    ]
    shares = lambda make: [make(side) for side in sides]
    scratch += shares(lambda side: vm((side.reduce, 2, side.group, side.cores * per_station, local), f32))
    scratch += shares(lambda side: vm((side.reduce, 2, h, stations), f32)) * 2
    scratch += shares(lambda side: vm((side.slots, blocks, stations), f32))
    scratch += shares(lambda side: vm((blocks, stations), f32))
    scratch += shares(lambda side: vm((side.group, side.cores * per_station, beams), f32))
    scratch += [vm((beams, stations), f32)] * 6
    scratch += shares(lambda side: vm((side.reduce, side.slots, h, lanes), f32))
    scratch += shares(lambda side: vm((side.reduce, side.slots, h, lanes), bf))
    scratch += shares(lambda side: vm((devices, h, lanes), bf))
    dma = pltpu.SemaphoreType.DMA
    scratch += [dma((SETS, deep, most))] * 2 + [dma((SETS, deep))] * 2 + [dma((SETS, most))] * 2
    scratch += [dma((SETS, deep, deep))] * 2 + [dma((SETS, deep, most, beams_local // piece))] * 2
    scratch += [dma((SETS, deep, most))] * 2
    scratch += [dma((SETS, deep, 2)), dma((SETS,)), dma((2,)), dma((SETS,)), dma((most,)), dma((2,))]
    scratch += [dma((3, deep)), dma((2,)), dma((2, SETS)), dma((2,))]
    results = pl.pallas_call(
        functools.partial(exchange_kernel, grid, n_taps, channels, radix),
        name="exchange",
        in_specs=[any_space] * 8,
        out_specs=[any_space] * len(outs),
        out_shape=outs,
        scratch_shapes=scratch,
        compiler_params=pltpu.CompilerParams(
            collective_id=0, has_side_effects=True, vmem_limit_bytes=VMEM_LIMIT
        ),
    )(voltages, *factors, *gains, delays, filter_taps, base)
    return results[0]


def times_unit(value, turn, radix):
    re, im = value
    quarter = turn * (4 // radix) % 4
    return ((re, im), (-im, re), (-re, -im), (im, -re))[quarter]


def combine(values, q):
    radix = len(values)
    re, im = values[0]
    for r in range(1, radix):
        more_re, more_im = times_unit(values[r], r * q, radix)
        re, im = re + more_re, im + more_im
    return re, im


def per_device(voltages, exponents, gain_real, gain_imag, delays, filter_taps):
    per_station, channels, lanes = voltages.shape
    devices = lax.axis_size("chan")
    local = channels // devices
    radix = radix_of(local // SETS)
    beams = delays.shape[1]
    grid = chip_grid(devices)
    rows, cols, cores = grid
    factor = jnp.exp2(exponents[:, :, 0].astype(jnp.float32)).astype(jnp.bfloat16).astype(jnp.float32)
    factors = []
    for s in range(SETS):
        side = Side(s, grid)
        e, r, k = side.place()
        here = lax.broadcasted_iota(jnp.int32, (1, side.slots, 1), 1) == e * cores + k
        placed = jnp.where(here, jnp.transpose(factor)[:, None, :], 0.0)
        factors.append(placed.reshape(factor.shape[1], side.slots * per_station))
    split = (rows, cols, cores * per_station)
    gains = [gain.reshape(*split, local) for gain in (gain_real, gain_imag)]
    return exchange(
        voltages, factors, gains, delays.reshape(*split, beams), filter_taps, grid, devices, beams, radix
    )


def solution(mesh):
    placed = (
        P("chan", None, "tm"),
        P("chan", None, "tm"),
        P(None, "chan"),
        P(None, "chan"),
        P(),
        P(),
    )
    return jax.shard_map(per_device, mesh=mesh, in_specs=placed, out_specs=P("chan", None, "tm"), check_vma=False)
```

time: 540 us -> 494 us (0.915)
  Pallas kernels: 523 us -> 478 us
  other arithmetic: 12 us -> 1.34 us
  local copies, waits for them, and re-layouts: 4.36 us -> 14.2 us
    pallas_call x1 -> x0, Pallas kernels: 58.4 us -> none  [synthesize(): pl.pallas_call(functools.partial(synthesis_kernel, radix), name='synthesi...]
    pallas_call x1, Pallas kernels: 464 us -> 478 us  [exchange(): pl.pallas_call(functools.partial(exchange_kernel, grid, n_taps, channels,...]
    unnamed x3 -> x1, local copies, waits for them, and re-layouts: 1.24 us -> 13.8 us
where the time goes in v1:
time: 494 us
  Pallas kernels  478 us (97%)
  local copies, waits for them, and re-layouts  14.2 us (3%)
    pallas_call x1, Pallas kernels, exchange(): pl.pallas_call(functools.partial(exchange_kernel, grid, n_taps, channels,...  478 us
    unnamed x1, local copies, waits for them, and re-layouts  13.8 us

profile of v1, /device:TPU:17, one launch (start us, length us, event | category | flops | bytes accessed | tf_op | source)
XLA Modules:
  0.0 493.9 jit_solution(5121603543188696669)
XLA Ops:
  0.0 0.1 broadcast_in_dim.41
  0.1 0.1 broadcast_in_dim.42
  0.2 0.1 broadcast_in_dim.47
  0.3 0.1 broadcast_in_dim.48
  0.3 0.7 convert_convert_fusion
  1.1 0.1 broadcast_in_dim.45
  1.2 0.6 broadcast_select_fusion
  1.8 478.3 %exchange.1 = (bf16[32,1024,256]{2,1,0:T(8,128)(2,1)}, bf16[8,32,64,256]{3,2,1,0:T(8,128)(2,1)}, bf16[8,32,64,256]{3,2,1,0:T(8,128)(2,1)}, bf16[2,4,64,64,256]{4...) custom-call(bf16[64,1024,256]{2,1,0:T(8,128)(2,1)} %refs_0_.1, ...), custom_call_target="tpu_custom_call" | custom-call | tf_op jit(solution)/shard_map/exchange/pallas_call | solution.py:723
  480.1 13.8 %copy.9 = bf16[32,1024,256]{2,1,0:T(8,128)(2,1)} copy(bf16[32,1024,256]{2,1,0:T(8,128)(2,1)} %get-tuple-element.6) | data formatting | bytes 33554432
  (3 shorter events, 0.0 us)

commit v2 on v1

--- a/solution.py
+++ b/solution.py
@@ -12,6 +12,7 @@
 TWO_PI = 6.283185307179586
 SETS = 2
 QUAD = 4
+ODD = 1
 VMEM_LIMIT = 60 * 1024 * 1024
 
 
@@ -51,20 +52,88 @@
         return e2 * self.cores + k2, self.device(e2, r, k2), e2, k2
 
 
+def times_unit(value, turn, radix):
+    re, im = value
+    quarter = turn * (4 // radix) % 4
+    return ((re, im), (-im, re), (-re, -im), (im, -re))[quarter]
+
+
+def combine(values, q):
+    radix = len(values)
+    re, im = values[0]
+    for r in range(1, radix):
+        more_re, more_im = times_unit(values[r], r * q, radix)
+        re, im = re + more_re, im + more_im
+    return re, im
+
+
+def transform(source, tab, partial, slot, r, per, half):
+    parts = [source(s, slice(r * per, (r + 1) * per)).reshape(-1, 2 * half) for s in range(SETS)]
+    x = jnp.concatenate(parts, axis=0)
+    turned = jnp.concatenate([-x[:, half:], x[:, :half]], axis=1)
+    both = jnp.concatenate([x, turned], axis=0)
+    partial[slot, r] = jnp.dot(tab[r], both, preferred_element_type=jnp.float32)
+
+
+def on_rows(partial, start, slot, store):
+    radix, span, lanes = partial.shape[1:]
+    half = lanes // 2
+    values = []
+    for r in range(radix):
+        both = partial[slot, r, pl.ds(start, 16), :]
+        values.append((both[:, :half], both[:, half:]))
+    for q in range(radix):
+        store(pl.ds(q * span + start, 16), combine(values, q))
+
+
+def one_beam(n, behind, xin, tab, taps, partial, before, oo, begin=True, end=True):
+    n_taps, _, half = taps.shape
+    radix, span = partial.shape[1:3]
+    per = xin.shape[3] // radix
+    lane = lax.broadcasted_iota(jnp.int32, (16, half), 1)
+    new, old = n % 2, (n + 1) % 2
+    shift = (half - n_taps * behind) % half
+
+    def store(at, signal):
+        for p in range(2):
+            cut = slice(p * half, (p + 1) * half)
+            total = taps[0, at, :] * signal[p]
+            for k in range(1, n_taps):
+                total = total + taps[k, at, :] * pltpu.roll(signal[p], k, 1)
+            total = total + jnp.where(lane < n_taps - 1, pltpu.roll(before[at, cut], shift, 1), 0.0)
+            oo[old, at, cut] = total.astype(oo.dtype)
+
+    for r in range(radix):
+        if begin:
+            transform(lambda s, at: xin[new, s, :, at, :], tab, partial, new, r, per, half)
+        if end:
+            for start in range(r * span // radix, (r + 1) * span // radix, 16):
+                on_rows(partial, start, old, store)
+
+
+def loop(low, high, work):
+    def body(n, carry):
+        work(n)
+        return carry
+
+    lax.fori_loop(low, high, body, 0)
+
+
 def exchange_kernel(grid, n_taps, channels, radix, *refs):
     sides = [Side(s, grid) for s in range(SETS)]
-    v, factors, gains, dl, ft, base = refs[0], refs[1:3], refs[3:5], refs[5], refs[6], refs[7]
-    out = refs[8]
-    spec, raw, part, got, done = (refs[9 + 2 * n : 11 + 2 * n] for n in range(5))
-    scratch = refs[19:]
+    v, powers, gains, dl, ft, base = refs[0], refs[1], refs[2:4], refs[4], refs[5], refs[6]
+    out, tab_out, taps_out, before_out = refs[7:11]
+    spec, raw, part, got, done = (refs[11 + 2 * n : 13 + 2 * n] for n in range(5))
+    scratch = refs[21:]
     xv, xf_re, xf_im, w_re, w_im, st_c, st_s, s_re, s_im, ob = scratch[:10]
     tab, taps, partial, before, xin, oo, ftv, basev = scratch[10:18]
     pa, pb = scratch[18:20]
-    pairs = (scratch[20 + 2 * n : 22 + 2 * n] for n in range(12))
-    gt, gsel, gbuf, fbuf, fsum, dtmp, dv, rot_c, rot_s, hal, hb, hv = pairs
-    sems = scratch[44:]
+    powers_in = scratch[20]
+    pairs = (scratch[21 + 2 * n : 23 + 2 * n] for n in range(13))
+    gt, gsel, gbuf, factors, fbuf, fsum, dtmp, dv, rot_c, rot_s, hal, hb, hv = pairs
+    sems = scratch[47:]
     raw_s, raw_r, gain_s, gain_r, fac_s, fac_r, part_s, part_r, fin_s, fin_r, end_s, end_r = sems[:12]
-    gain_in, delay_in, extra_in, own_in, load_in, out_sem, fetch_in, put_sem, x_in, o_out = sems[12:]
+    gain_in, delay_in, extra_in, load_in, out_sem, fetch_in, put_sem, x_in, o_out, keep_sem = sems[12:]
 
     per_station, _, lanes = v.shape
     half = lanes // 2
@@ -79,8 +148,10 @@
     groups = lax.axis_size("tm")
     tm = lax.axis_index("tm")
     block = ob.shape[1]
+    lift, high = xf_re.shape[0] // stations, s_re.shape[0] // beams
     piece = beams_local // fin_s.shape[3]
     pieces = beams_local // piece
+    ready = out.shape[0]
     early = max(1, 5 * pieces // 8)
     width = channels // fsum[0].shape[0]
     me = lax.axis_index("chan")
@@ -197,37 +268,35 @@
                 for off in range(1, side.cores):
                     raw_copy(side, u, off).start()
 
-    def loop(low, high, work):
-        def body(n, carry):
-            work(n)
-            return carry
-
-        lax.fori_loop(low, high, body, 0)
-
     def aligned(n, size):
         return pl.ds(pl.multiple_of(n * size, size), size)
 
     start_raw(0)
-    gain_loads, delay_loads, extra_loads, own_loads = [], [], [], []
+    gain_loads, delay_loads = [], []
     for side in sides:
         s = side.which
         e, r, k = side.place()
-        for off in range(1, side.slots):
-            factor_copy(side, off).start()
         for r2 in range(side.reduce):
             for p in range(2):
                 source = span_of(side, gains[p], r2)
                 gain_loads.append(pltpu.make_async_copy(source, gt[s].at[r2, p], gain_in.at[s, r2, p]))
         delay_loads.append(pltpu.make_async_copy(span_of(side, dl, r), dtmp[s], delay_in.at[s]))
-        own_loads.append(pltpu.make_async_copy(factors[s], fbuf[s].at[e * side.cores + k], own_in.at[s]))
-    extra_loads = [pltpu.make_async_copy(ft, ftv, extra_in.at[0]), pltpu.make_async_copy(base, basev, extra_in.at[1])]
-    loads = gain_loads + delay_loads + own_loads + extra_loads
+    extra = ((powers, powers_in), (ft, ftv), (base, basev))
+    loads = [pltpu.make_async_copy(one, two, extra_in.at[n]) for n, (one, two) in enumerate(extra)]
+    loads += gain_loads + delay_loads
     for load in loads:
         load.start()
     for load in loads:
         load.wait()
+    power = jnp.exp2(powers_in[...].astype(jnp.float32)).astype(jnp.bfloat16).astype(jnp.float32)
     for side in sides:
         s = side.which
+        e, r, k = side.place()
+        mine = e * side.cores + k
+        placed = jnp.transpose(jnp.concatenate([power] * side.slots, axis=0))
+        place = lax.broadcasted_iota(jnp.int32, placed.shape, 1) // per_station
+        factors[s][...] = jnp.where(place == mine, placed, 0.0)
+        fbuf[s][mine] = factors[s][...]
         for r2 in range(side.reduce):
             for p in range(2):
                 turned = jnp.transpose(gt[s][r2, p].reshape(stations, local))
@@ -243,6 +312,8 @@
                 at = (i * cols + j) * held
                 dv[s][to : to + held, :] = turned[at : at + held]
     for side in sides:
+        for off in range(1, side.slots):
+            factor_copy(side, off).start()
         for d in range(1, side.reduce):
             gain_copy(side, d).start()
     for u in range(1, max(side.reduce for side in sides)):
@@ -327,11 +398,11 @@
 
         def tile(t):
             def spread(n):
-                x = xv[aligned(n, 16), aligned(t, 16), :]
-                x = x.astype(jnp.float32).reshape(256, lanes)
-                at = aligned(n, 256)
-                xf_re[at, :] = x[:, :half]
-                xf_im[at, :] = x[:, half:]
+                x = xv[aligned(n, 16), aligned(t, 16), :].astype(jnp.float32)
+                for i in range(16):
+                    at = pl.ds((n * 16 + i) * lift, 16)
+                    xf_re[at, :] = x[i, :, :half]
+                    xf_im[at, :] = x[i, :, half:]
 
             loop(0, stations // 16, spread)
 
@@ -355,12 +426,12 @@
 
                 loop(0, beams // 16, weigh)
                 for q in range(QUAD):
-                    from_rows = pl.ds(g * QUAD + q, stations, stride=16)
+                    from_rows = pl.ds(g * QUAD + q, stations, stride=lift)
                     x = jnp.concatenate([xf_re[from_rows, :], xf_im[from_rows, :]], axis=1).astype(jnp.bfloat16)
                     real = jnp.dot(w_re[q], x, preferred_element_type=jnp.float32)
                     imag = jnp.dot(w_im[q], x, preferred_element_type=jnp.float32)
                     c = c0 + q
-                    to_rows = pl.ds(c % radix * per + c // radix, beams, stride=h)
+                    to_rows = pl.ds(c % radix * per + c // radix, beams, stride=high)
                     s_re[to_rows, :] = real[:, :half] - imag[:, half:]
                     s_im[to_rows, :] = real[:, half:] + imag[:, :half]
 
@@ -379,9 +450,10 @@
             def _():
                 put(n - 2).wait()
 
-            at = aligned(n, block * h)
-            ob[n % 2, :, :, :half] = s_re[at, :].reshape(block, h, half).astype(ob.dtype)
-            ob[n % 2, :, :, half:] = s_im[at, :].reshape(block, h, half).astype(ob.dtype)
+            for i in range(block):
+                at = pl.ds((n * block + i) * high, h)
+                ob[n % 2, i, :, :half] = s_re[at, :].astype(ob.dtype)
+                ob[n % 2, i, :, half:] = s_im[at, :].astype(ob.dtype)
             put(n).start()
 
         loop(0, beams // block, flush)
@@ -529,24 +601,8 @@
                     end_copy(side, u, off).wait_recv()
 
     lane = lax.broadcasted_iota(jnp.int32, (16, half), 1)
-
-    def transform(source, slot, r):
-        parts = [source(s, slice(r * per, (r + 1) * per)).reshape(-1, lanes) for s in range(SETS)]
-        x = jnp.concatenate(parts, axis=0)
-        turned = jnp.concatenate([-x[:, half:], x[:, :half]], axis=1)
-        both = jnp.concatenate([x, turned], axis=0)
-        partial[slot, r] = jnp.dot(tab[r], both, preferred_element_type=jnp.float32)
-
-    def on_rows(start, slot, store):
-        values = []
-        for r in range(radix):
-            both = partial[slot, r, pl.ds(start, 16), :]
-            values.append((both[:, :half], both[:, half:]))
-        for q in range(radix):
-            store(pl.ds(q * span + start, 16), combine(values, q))
-
     for r in range(radix):
-        transform(lambda s, at: hv[s][:, at, :], 1, r)
+        transform(lambda s, at: hv[s][:, at, :], tab, partial, 1, r, per, half)
     frame = lane % n_taps
 
     def keep_before(at, signal):
@@ -559,7 +615,14 @@
                 total = total + jnp.where(frame < k, tap * moved, 0.0)
             before[at, p * half : (p + 1) * half] = total
 
-    loop(0, span // 16, lambda n: on_rows(pl.multiple_of(n * 16, 16), 1, keep_before))
+    loop(0, span // 16, lambda n: on_rows(partial, pl.multiple_of(n * 16, 16), 1, keep_before))
+    kept = [
+        pltpu.make_async_copy(tab, tab_out, keep_sem.at[0]),
+        pltpu.make_async_copy(taps, taps_out, keep_sem.at[1]),
+        pltpu.make_async_copy(before, before_out, keep_sem.at[2]),
+    ]
+    for copy in kept:
+        copy.start()
 
     def fetch_beam(n):
         return [
@@ -580,12 +643,12 @@
         copy.start()
 
     def synthesize(n):
-        @pl.when(n < beams_local)
+        @pl.when(n < ready)
         def _():
             for copy in fetch_beam(n):
                 copy.wait()
 
-        more = jnp.logical_and((n + 1) % piece > 0, n + 1 < beams_local)
+        more = jnp.logical_and((n + 1) % piece > 0, n + 1 < ready)
 
         @pl.when(more)
         def _():
@@ -596,36 +659,24 @@
         def _():
             send_out(n - 3).wait()
 
-        new, old = n % 2, (n + 1) % 2
-        shift = (half - n_taps * jnp.maximum(n - 1, 0)) % half
-
-        def store(at, signal):
-            for p in range(2):
-                cut = slice(p * half, (p + 1) * half)
-                total = taps[0, at, :] * signal[p]
-                for k in range(1, n_taps):
-                    total = total + taps[k, at, :] * pltpu.roll(signal[p], k, 1)
-                total = total + jnp.where(lane < tail, pltpu.roll(before[at, cut], shift, 1), 0.0)
-                oo[old, at, cut] = total.astype(oo.dtype)
-
-        for r in range(radix):
-            transform(lambda s, at: xin[new, s, :, at, :], new, r)
-            for start in range(r * span // radix, (r + 1) * span // radix, 16):
-                on_rows(start, old, store)
+        one_beam(n, jnp.maximum(n - 1, 0), xin, tab, taps, partial, before, oo)
 
         @pl.when(n >= 1)
         def _():
             send_out(n - 1).start()
 
-        @pl.when(jnp.logical_and((n + 1) % piece == 0, n + 1 < beams_local))
+        @pl.when(jnp.logical_and((n + 1) % piece == 0, n + 1 < ready))
         def _():
             arrive((n + 1) // piece)
             for copy in fetch_beam(n + 1):
                 copy.start()
 
-    loop(0, beams_local + 1, synthesize)
-    for n in range(max(0, beams_local - 2), beams_local):
+    loop(0, ready + 1, synthesize)
+    arrive(pieces - 1)
+    for n in range(max(0, ready - 2), ready):
         send_out(n).wait()
+    for copy in kept:
+        copy.wait()
 
     for side in sides:
         for off in range(1, side.slots):
@@ -657,12 +708,12 @@
     return jnp.asarray(np.broadcast_to(channel, (8, span)), jnp.int32)
 
 
-def exchange(voltages, factors, gains, delays, filter_taps, grid, devices, beams, radix):
+def exchange(voltages, powers, gains, delays, filter_taps, grid, devices, beams, radix):
     per_station, channels, lanes = voltages.shape
     half = lanes // 2
     n_taps = filter_taps.shape[0]
     sides = [Side(s, grid) for s in range(SETS)]
-    stations = factors[0].shape[1]
+    stations = max(side.slots for side in sides) * per_station
     beams_local = beams // devices
     local = channels // devices
     h = local // SETS
@@ -673,25 +724,30 @@
     deep = max(side.reduce for side in sides)
     bf, f32 = jnp.bfloat16, jnp.float32
     hbm = lambda *shape: jax.ShapeDtypeStruct(shape, bf)
-    outs = [hbm(beams_local, channels, lanes)]
+    outs = [
+        hbm(beams_local - piece, channels, lanes),
+        hbm(radix, span, 2 * span),
+        jax.ShapeDtypeStruct((n_taps, channels, half), f32),
+        jax.ShapeDtypeStruct((channels, lanes), f32),
+    ]
     outs += [hbm(devices, beams_local, h, lanes)] * 2
     outs += [hbm(side.reduce, side.slots, per_station, h, lanes) for side in sides]
     outs += [hbm(side.reduce, side.reduce, side.slots * beams_local, h, lanes) for side in sides] * 2
     outs += [hbm(side.reduce, side.slots, beams_local, h, lanes) for side in sides]
     any_space = pl.BlockSpec(memory_space=pl.ANY)
     vm = pltpu.VMEM
-    blocks = factors[0].shape[0]
+    blocks = powers.shape[1]
     base = place_map(channels, devices, h, radix)
     scratch = [
         vm((stations, h, lanes), bf),
-        vm((stations * 16, half), f32),
-        vm((stations * 16, half), f32),
+        vm((stations * (16 + ODD), half), f32),
+        vm((stations * (16 + ODD), half), f32),
         vm((QUAD, beams, stations), bf),
         vm((QUAD, beams, stations), bf),
         vm((beams, stations), f32),
         vm((beams, stations), f32),
-        vm((beams * h, half), f32),
-        vm((beams * h, half), f32),
+        vm((beams * (h + ODD), half), f32),
+        vm((beams * (h + ODD), half), f32),
         vm((2, block, h, lanes), bf),
         vm((radix, span, 2 * span), bf),
         vm((n_taps, channels, half), f32),
@@ -703,10 +759,12 @@
         vm(base.shape, jnp.int32),
         vm((3, deep, block, h, lanes), bf),
         vm((2, block, h, lanes), bf),
+        vm(powers.shape, jnp.int32),
     ]
     shares = lambda make: [make(side) for side in sides]
     scratch += shares(lambda side: vm((side.reduce, 2, side.group, side.cores * per_station, local), f32))
     scratch += shares(lambda side: vm((side.reduce, 2, h, stations), f32)) * 2
+    scratch += shares(lambda side: vm((blocks, stations), f32))
     scratch += shares(lambda side: vm((side.slots, blocks, stations), f32))
     scratch += shares(lambda side: vm((blocks, stations), f32))
     scratch += shares(lambda side: vm((side.group, side.cores * per_station, beams), f32))
@@ -718,35 +776,97 @@
     scratch += [dma((SETS, deep, most))] * 2 + [dma((SETS, deep))] * 2 + [dma((SETS, most))] * 2
     scratch += [dma((SETS, deep, deep))] * 2 + [dma((SETS, deep, most, beams_local // piece))] * 2
     scratch += [dma((SETS, deep, most))] * 2
-    scratch += [dma((SETS, deep, 2)), dma((SETS,)), dma((2,)), dma((SETS,)), dma((most,)), dma((2,))]
-    scratch += [dma((3, deep)), dma((2,)), dma((2, SETS)), dma((2,))]
+    scratch += [dma((SETS, deep, 2)), dma((SETS,)), dma((3,)), dma((most,)), dma((2,))]
+    scratch += [dma((3, deep)), dma((2,)), dma((2, SETS)), dma((2,)), dma((3,))]
     results = pl.pallas_call(
         functools.partial(exchange_kernel, grid, n_taps, channels, radix),
         name="exchange",
-        in_specs=[any_space] * 8,
+        in_specs=[any_space] * 7,
         out_specs=[any_space] * len(outs),
         out_shape=outs,
         scratch_shapes=scratch,
         compiler_params=pltpu.CompilerParams(
             collective_id=0, has_side_effects=True, vmem_limit_bytes=VMEM_LIMIT
         ),
-    )(voltages, *factors, *gains, delays, filter_taps, base)
-    return results[0]
-
-
-def times_unit(value, turn, radix):
-    re, im = value
-    quarter = turn * (4 // radix) % 4
-    return ((re, im), (-im, re), (-re, -im), (im, -re))[quarter]
-
-
-def combine(values, q):
-    radix = len(values)
-    re, im = values[0]
-    for r in range(1, radix):
-        more_re, more_im = times_unit(values[r], r * q, radix)
-        re, im = re + more_re, im + more_im
-    return re, im
+    )(voltages, powers, *gains, delays, filter_taps, base)
+    return conclude(*results[:6], beams_local)
+
+
+def conclude_kernel(res, tab_in, taps_in, before_in, spec_a, spec_b, out, *scratch):
+    tab, taps, before, xin, partial, oo, held, const_in, x_in, o_out, in_sem, out_sem = scratch
+    spec = (spec_a, spec_b)
+    first = res.shape[0]
+    last = out.shape[0] - first
+    size = held.shape[1]
+    chunks = held.shape[0]
+
+    def fetch_beam(n):
+        return [pltpu.make_async_copy(spec[s].at[:, first + n], xin.at[n % 2, s], x_in.at[n % 2, s]) for s in range(SETS)]
+
+    def send_out(n):
+        return pltpu.make_async_copy(oo.at[n % 2], out.at[first + n], o_out.at[n % 2])
+
+    consts = ((tab_in, tab), (taps_in, taps), (before_in, before))
+    loads = [pltpu.make_async_copy(one, two, const_in.at[n]) for n, (one, two) in enumerate(consts)]
+    takes = [pltpu.make_async_copy(res.at[pl.ds(c * size, size)], held.at[c], in_sem.at[c]) for c in range(chunks)]
+    gives = [pltpu.make_async_copy(held.at[c], out.at[pl.ds(c * size, size)], out_sem.at[c]) for c in range(chunks)]
+    for copy in fetch_beam(0) + loads + takes:
+        copy.start()
+    for copy in loads:
+        copy.wait()
+    moved = 0
+    for n in range(last + 1):
+        if n < last:
+            for copy in fetch_beam(n):
+                copy.wait()
+        if n + 1 < last:
+            for copy in fetch_beam(n + 1):
+                copy.start()
+        if n >= 3:
+            send_out(n - 3).wait()
+        one_beam(n, first + n - 1, xin, tab, taps, partial, before, oo, n < last, n > 0)
+        if n >= 1:
+            send_out(n - 1).start()
+        upto = min(chunks, -(-chunks * (n + 1) // last))
+        for c in range(moved, upto):
+            takes[c].wait()
+            gives[c].start()
+        moved = max(moved, upto)
+    for n in range(max(0, last - 2), last):
+        send_out(n).wait()
+    for copy in gives:
+        copy.wait()
+
+
+def conclude(res, tab, taps, before, spec_a, spec_b, beams_local):
+    first, channels, lanes = res.shape
+    devices, _, h, _ = spec_a.shape
+    radix, span = tab.shape[:2]
+    size = math.gcd(first, 4)
+    vm, dma = pltpu.VMEM, pltpu.SemaphoreType.DMA
+    any_space = pl.BlockSpec(memory_space=pl.ANY)
+    return pl.pallas_call(
+        conclude_kernel,
+        name="conclude",
+        in_specs=[any_space] * 6,
+        out_specs=any_space,
+        out_shape=jax.ShapeDtypeStruct((beams_local, channels, lanes), jnp.bfloat16),
+        scratch_shapes=[
+            vm(tab.shape, tab.dtype),
+            vm(taps.shape, taps.dtype),
+            vm(before.shape, before.dtype),
+            vm((2, SETS, devices, h, lanes), jnp.bfloat16),
+            vm((2, radix, span, lanes), jnp.float32),
+            vm((2, channels, lanes), jnp.bfloat16),
+            vm((first // size, size, channels, lanes), jnp.bfloat16),
+            dma((3,)),
+            dma((2, SETS)),
+            dma((2,)),
+            dma((first // size,)),
+            dma((first // size,)),
+        ],
+        compiler_params=pltpu.CompilerParams(vmem_limit_bytes=VMEM_LIMIT),
+    )(res, tab, taps, before, spec_a, spec_b)
 
 
 def per_device(voltages, exponents, gain_real, gain_imag, delays, filter_taps):
@@ -757,18 +877,10 @@
     beams = delays.shape[1]
     grid = chip_grid(devices)
     rows, cols, cores = grid
-    factor = jnp.exp2(exponents[:, :, 0].astype(jnp.float32)).astype(jnp.bfloat16).astype(jnp.float32)
-    factors = []
-    for s in range(SETS):
-        side = Side(s, grid)
-        e, r, k = side.place()
-        here = lax.broadcasted_iota(jnp.int32, (1, side.slots, 1), 1) == e * cores + k
-        placed = jnp.where(here, jnp.transpose(factor)[:, None, :], 0.0)
-        factors.append(placed.reshape(factor.shape[1], side.slots * per_station))
     split = (rows, cols, cores * per_station)
     gains = [gain.reshape(*split, local) for gain in (gain_real, gain_imag)]
     return exchange(
-        voltages, factors, gains, delays.reshape(*split, beams), filter_taps, grid, devices, beams, radix
+        voltages, exponents[:, :, 0], gains, delays.reshape(*split, beams), filter_taps, grid, devices, beams, radix
     )
 
 

time: 494 us -> 481 us (0.974)
  local copies, waits for them, and re-layouts: 14.2 us -> 1.39 us
    pallas_call x0 -> x1, Pallas kernels: none -> 13.3 us  [conclude(): pl.pallas_call(conclude_kernel, name='conclude', in_specs=[any_space] * 6...]
    pallas_call x1, Pallas kernels: 478 us -> 465 us  [exchange(): pl.pallas_call(functools.partial(exchange_kernel, grid, n_taps, channels,...]
    unnamed x1, local copies, waits for them, and re-layouts: 13.8 us -> 1.39 us
where the time goes in v2:
time: 481 us; the launch traced here: 480 us
  Pallas kernels  479 us (100%)
    pallas_call x1, Pallas kernels, exchange(): pl.pallas_call(functools.partial(exchange_kernel, grid, n_taps, channels,...  465 us
    pallas_call x1, Pallas kernels, conclude(): pl.pallas_call(conclude_kernel, name='conclude', in_specs=[any_space] * 6...  13.3 us

profile of v2, /device:TPU:17, one launch (start us, length us, event | category | flops | bytes accessed | tf_op | source)
XLA Modules:
  0.0 480.1 jit_solution(9173797598848342604)
XLA Ops:
  0.0 1.4 copy.8
  1.4 465.4 %exchange.1 = (bf16[28,1024,256]{2,1,0:T(8,128)(2,1)}, bf16[4,256,512]{2,1,0:T(8,128)(2,1)}, f32[4,1024,128]{2,1,0:T(8,128)}, f32[1024,256]{1,0:T(8,128)}, bf16[...) custom-call(bf16[64,1024,256]{2,1,0:T(8,128)(2,1)} %refs_0_.1, ...), custom_call_target="tpu_custom_call" | custom-call | tf_op jit(solution)/shard_map/exchange/pallas_call | solution.py:781
  466.8 13.3 %conclude.1 = bf16[32,1024,256]{2,1,0:T(8,128)(2,1)} custom-call(bf16[28,1024,256]{2,1,0:T(8,128)(2,1)} %get-tuple-element.11.res, bf16[4,256,512]{2,1,0:T(8,128)(2,1)} %get-tuple-element.12.tab_in, f32[4,1024,128]{2,1,0:T(8,128)} %get-tuple-element.13.taps_in, f32[1024,256]{1,0:T(8,128)} %get-tuple-element.14.before_in, ...), custom_call_target="tpu_custom_call" | custom-call | tf_op jit(solution)/shard_map/conclude/pallas_call | solution.py:848

commit v3 on v2

--- a/solution.py
+++ b/solution.py
@@ -293,9 +293,10 @@
         s = side.which
         e, r, k = side.place()
         mine = e * side.cores + k
-        placed = jnp.transpose(jnp.concatenate([power] * side.slots, axis=0))
-        place = lax.broadcasted_iota(jnp.int32, placed.shape, 1) // per_station
-        factors[s][...] = jnp.where(place == mine, placed, 0.0)
+        place = lax.broadcasted_iota(jnp.int32, (1, stations), 1) // per_station
+        for n in range(powers.shape[0]):
+            placed = jnp.concatenate([power[n]] * side.slots, axis=1)
+            factors[s][n : n + 1, :] = jnp.where(place == mine, placed, 0.0)
         fbuf[s][mine] = factors[s][...]
         for r2 in range(side.reduce):
             for p in range(2):
@@ -648,10 +649,12 @@
             for copy in fetch_beam(n):
                 copy.wait()
 
-        more = jnp.logical_and((n + 1) % piece > 0, n + 1 < ready)
-
-        @pl.when(more)
+        @pl.when(n + 1 < ready)
         def _():
+            @pl.when((n + 1) % piece == 0)
+            def _():
+                arrive((n + 1) // piece)
+
             for copy in fetch_beam(n + 1):
                 copy.start()
 
@@ -664,12 +667,6 @@
         @pl.when(n >= 1)
         def _():
             send_out(n - 1).start()
-
-        @pl.when(jnp.logical_and((n + 1) % piece == 0, n + 1 < ready))
-        def _():
-            arrive((n + 1) // piece)
-            for copy in fetch_beam(n + 1):
-                copy.start()
 
     loop(0, ready + 1, synthesize)
     arrive(pieces - 1)
@@ -736,7 +733,7 @@
     outs += [hbm(side.reduce, side.slots, beams_local, h, lanes) for side in sides]
     any_space = pl.BlockSpec(memory_space=pl.ANY)
     vm = pltpu.VMEM
-    blocks = powers.shape[1]
+    blocks = powers.shape[0]
     base = place_map(channels, devices, h, radix)
     scratch = [
         vm((stations, h, lanes), bf),
@@ -880,7 +877,7 @@
     split = (rows, cols, cores * per_station)
     gains = [gain.reshape(*split, local) for gain in (gain_real, gain_imag)]
     return exchange(
-        voltages, exponents[:, :, 0], gains, delays.reshape(*split, beams), filter_taps, grid, devices, beams, radix
+        voltages, jnp.transpose(exponents, (1, 2, 0)), gains, delays.reshape(*split, beams), filter_taps, grid, devices, beams, radix
     )
 
 

time: 481 us -> 479 us (level)
  no operation moved by 1% of the time
where the time goes in v3:
time: 479 us
  Pallas kernels  479 us (100%)
    pallas_call x1, Pallas kernels, exchange(): pl.pallas_call(functools.partial(exchange_kernel, grid, n_taps, channels,...  465 us
    pallas_call x1, Pallas kernels, conclude(): pl.pallas_call(conclude_kernel, name='conclude', in_specs=[any_space] * 6...  13.3 us

profile of v3, /device:TPU:17, one launch (start us, length us, event | category | flops | bytes accessed | tf_op | source)
XLA Modules:
  0.0 478.7 jit_solution(9444420553295279606)
XLA Ops:
  0.0 465.4 %exchange.1 = (bf16[28,1024,256]{2,1,0:T(8,128)(2,1)}, bf16[4,256,512]{2,1,0:T(8,128)(2,1)}, f32[4,1024,128]{2,1,0:T(8,128)}, f32[1024,256]{1,0:T(8,128)}, bf16[...) custom-call(bf16[64,1024,256]{2,1,0:T(8,128)(2,1)} %refs_0_.1, ...), custom_call_target="tpu_custom_call" | custom-call | tf_op jit(solution)/shard_map/exchange/pallas_call | solution.py:778
  465.4 13.3 %conclude.1 = bf16[32,1024,256]{2,1,0:T(8,128)(2,1)} custom-call(bf16[28,1024,256]{2,1,0:T(8,128)(2,1)} %get-tuple-element.11.res, bf16[4,256,512]{2,1,0:T(8,128)(2,1)} %get-tuple-element.12.tab_in, f32[4,1024,128]{2,1,0:T(8,128)} %get-tuple-element.13.taps_in, f32[1024,256]{1,0:T(8,128)} %get-tuple-element.14.before_in, ...), custom_call_target="tpu_custom_call" | custom-call | tf_op jit(solution)/shard_map/conclude/pallas_call | solution.py:845
